TPU v7x, 32 devices: a whole 2x2x4 slice. The times are simulated.
32 devices in a mesh: rep: 4 (over y, x), seq: 8 (over z, core).
Axes of the slice: x: 2, y: 2, z: 4, core: 2. Of those that a mesh axis runs over, the one named last changes fastest.
Arguments:
- inputs: bfloat16 [4, 2048, 1536], P('rep', 'seq'), may hold values from -13 to 13
- segment_ids: int32 [4, 2048], P('rep'), may hold values from 0 to 7, as said below
- valid_mask: int32 [4, 2048], P('rep'), may hold values from 0 to 1, as said below
- input_weight: bfloat16 [1536, 4608], P('seq'), may hold values from -0.15625 to 0.15625
- output_weight: bfloat16 [1536, 1536], P('seq'), may hold values from -0.15625 to 0.15625
- conv_kernel: float32 [16, 6, 11], replicated, may hold values from -1.2 to 1.2
- head_mix: float32 [8, 2, 2], replicated, may hold values from 0.2 to 1
- first_gain: float32 [1536], replicated, may hold values from 0.5 to 1.5
- second_gain: float32 [1536], replicated, may hold values from 0.5 to 1.5
- group_gain: float32 [1536], replicated, may hold values from 0.5 to 1.5
- gate_weight: bfloat16 [1536, 4096], P(None, 'seq'), may hold values from -0.15625 to 0.15625
- up_weight: bfloat16 [1536, 4096], P(None, 'seq'), may hold values from -0.15625 to 0.15625
- down_weight: bfloat16 [4096, 1536], P('seq'), may hold values from -0.09375 to 0.09375
- cotangent: bfloat16 [4, 2048, 1536], P('rep', 'seq'), may hold values from -17 to 17
Outputs:
- output: bfloat16 [4, 2048, 1536], P('rep', 'seq')
- grad_inputs: bfloat16 [4, 2048, 1536], P('rep', 'seq')
- grad_input_weight: float32 [1536, 4608], P('seq')
- grad_output_weight: float32 [1536, 1536], P('seq')
- grad_kernel: float32 [16, 6, 11], replicated
- grad_mix: float32 [8, 2, 2], replicated
- grad_first_gain: float32 [1536], replicated
- grad_second_gain: float32 [1536], replicated
- grad_group_gain: float32 [1536], replicated
- grad_gate: float32 [1536, 4096], P(None, 'seq')
- grad_up: float32 [1536, 4096], P(None, 'seq')
- grad_down: float32 [4096, 1536], P('seq')
Inputs may be any that keep to these rules, and one draw needn't show every extreme that they name: `segment_ids`: segment ids never fall along a sequence and start at 0. The positions k * 1024 to (k + 1) * 1024 - 1 form frame k; every document lies inside one frame, a frame holds one to four documents, the first frame of the first sequence is a single document of exactly 1024 positions, and every frame of the last sequence holds four documents. `valid_mask`: in each frame the positions with 0 form its tail, at most 256 of them; the first frame of the first sequence has none.
All inputs are finite; a program needn't handle non-finite values.
Results may differ from a plain program's by a relative error of at most 0.02.
Values may be sent and summed in bfloat16 or wider, within the bound.
A program may use at most 384 MiB of HBM per device.

v0:
```python
import jax
import jax.numpy as jnp
from jax import lax
from jax.sharding import PartitionSpec as P

REACH = 4
EPS = 1e-06
HIGHEST = lax.Precision.HIGHEST


def from_behind(x, axis, by):
    count = lax.axis_size(axis)
    pairs = [(i, i + by) for i in range(count) if 0 <= i + by < count]
    return lax.ppermute(x, axis, pairs)


def convolve(logits, kernel, rows, columns):
    rim_rows = kernel.shape[1] - 1
    key_span = kernel.shape[2] - 1
    result = jnp.zeros((logits.shape[0], rows, columns), jnp.float32)
    for row_tap in range(kernel.shape[1]):
        for col_tap in range(kernel.shape[2]):
            weight = kernel[:, row_tap, col_tap][:, None, None]
            result = (
                result
                + weight
                * logits[
                    :,
                    rim_rows - row_tap : rim_rows - row_tap + rows,
                    key_span - col_tap : key_span - col_tap + columns,
                ]
            )
    return result


def convolve_back(grads, kernel):
    rim_rows = kernel.shape[1] - 1
    key_span = kernel.shape[2] - 1
    rows = grads.shape[1] + rim_rows
    columns = grads.shape[2] + key_span
    padded = jnp.pad(grads, ((0, 0), (rim_rows, rim_rows), (key_span, key_span)))
    result = jnp.zeros((grads.shape[0], rows, columns), jnp.float32)
    for row_tap in range(kernel.shape[1]):
        for col_tap in range(kernel.shape[2]):
            weight = kernel[:, row_tap, col_tap][:, None, None]
            result = (
                result + weight * padded[:, row_tap : row_tap + rows, col_tap : col_tap + columns]
            )
    return result


def kernel_grads(grads, logits, taps_rows, taps_cols):
    rim_rows = taps_rows - 1
    key_span = taps_cols - 1
    rows = grads.shape[1]
    columns = grads.shape[2]
    entries = []
    for row_tap in range(taps_rows):
        line_sums = []
        for col_tap in range(taps_cols):
            window_part = logits[
                :,
                rim_rows - row_tap : rim_rows - row_tap + rows,
                key_span - col_tap : key_span - col_tap + columns,
            ]
            line_sums.append(jnp.sum(grads * window_part, axis=(1, 2)))
        entries.append(jnp.stack(line_sums, axis=-1))
    return jnp.stack(entries, axis=1)


def attend_group(operands, mask_ext, mask_own, row_valid, score_scale):
    query_g, key_g, value_g, kernel_g, mixing_g = operands
    rows = mask_own.shape[0]
    columns = mask_own.shape[1]
    raw = jnp.einsum("qhd,khd->hqk", query_g, key_g, preferred_element_type=jnp.float32)
    logits = raw * score_scale * mask_ext
    conv = convolve(logits, kernel_g, rows, columns)
    allowed = mask_own > 0
    peak = jnp.max(jnp.where(allowed, conv, -1e30), axis=-1, keepdims=True)
    peak = jnp.where(row_valid > 0, peak, 0.0)
    expo = jnp.where(allowed, jnp.exp(conv - peak), 0.0)
    denom = jnp.sum(expo, axis=-1, keepdims=True) + 1.0 - row_valid
    prob = expo / denom
    mixed = (
        mixing_g[:, 0][:, None, None] * prob[0][None]
        + mixing_g[:, 1][:, None, None] * prob[1][None]
    )
    mixed_low = mixed.astype(jnp.bfloat16)
    result = jnp.einsum("hqk,khd->qhd", mixed_low, value_g, preferred_element_type=jnp.float32)
    return (result, peak + jnp.log(denom))


def attend_group_back(operands, mask_ext, mask_own, score_scale):
    query_g, key_g, value_g, kernel_g, mixing_g, dresult_g, lse_g = operands
    rows = mask_own.shape[0]
    columns = mask_own.shape[1]
    raw = jnp.einsum("qhd,khd->hqk", query_g, key_g, preferred_element_type=jnp.float32)
    logits = raw * score_scale * mask_ext
    conv = convolve(logits, kernel_g, rows, columns)
    allowed = mask_own > 0
    prob = jnp.where(allowed, jnp.exp(conv - lse_g), 0.0)
    mixed = (
        mixing_g[:, 0][:, None, None] * prob[0][None]
        + mixing_g[:, 1][:, None, None] * prob[1][None]
    )
    mixed_low = mixed.astype(jnp.bfloat16)
    dmixed = jnp.einsum("qhd,khd->hqk", dresult_g, value_g, preferred_element_type=jnp.float32)
    dvalue = jnp.einsum("hqk,qhd->khd", mixed_low, dresult_g, preferred_element_type=jnp.float32)
    dmixing = jnp.stack(
        [
            jnp.sum(dmixed * prob[0][None], axis=(1, 2)),
            jnp.sum(dmixed * prob[1][None], axis=(1, 2)),
        ],
        axis=-1,
    )
    dprob = (
        mixing_g[0][:, None, None] * dmixed[0][None] + mixing_g[1][:, None, None] * dmixed[1][None]
    )
    dconv = prob * (dprob - jnp.sum(prob * dprob, axis=-1, keepdims=True))
    dkernel = kernel_grads(dconv, logits, kernel_g.shape[1], kernel_g.shape[2])
    dlogits = convolve_back(dconv, kernel_g) * mask_ext * score_scale
    dquery = jnp.einsum(
        "hqk,khd->qhd",
        dlogits,
        key_g.astype(jnp.float32),
        precision=HIGHEST,
        preferred_element_type=jnp.float32,
    )
    dkey = jnp.einsum(
        "hqk,qhd->khd",
        dlogits,
        query_g.astype(jnp.float32),
        precision=HIGHEST,
        preferred_element_type=jnp.float32,
    )
    return (dquery, dkey, dvalue, dkernel, dmixing)


def rms_scale(values):
    return lax.rsqrt(jnp.mean(values * values, axis=-1, keepdims=True) + EPS)


def norm_back(grad_out, values, inv_scale, gain):
    scaled_grad = grad_out * gain
    inner = jnp.mean(scaled_grad * values, axis=-1, keepdims=True)
    return inv_scale * scaled_grad - values * inv_scale**3 * inner


def on_device(
    inputs,
    segment_ids,
    valid_mask,
    input_weight,
    output_weight,
    conv_kernel,
    head_mix,
    first_gain,
    second_gain,
    group_gain,
    gate_weight,
    up_weight,
    down_weight,
    cotangent,
):
    tokens = inputs.shape[1]
    model_width = inputs.shape[2]
    head_count = conv_kernel.shape[0]
    head_dim = model_width // head_count
    groups = head_mix.shape[0]
    rim_rows = conv_kernel.shape[1] - 1
    half_span = conv_kernel.shape[2] // 2
    window = REACH * tokens
    score_scale = head_dim ** (-0.5)
    seq_rank = lax.axis_index("seq")
    row_start = seq_rank * tokens
    window_start = row_start - (REACH - 1) * tokens
    resid_in = inputs[0].astype(jnp.float32)
    grad_out = cotangent[0].astype(jnp.float32)
    offset = window + half_span
    segment_pad = jnp.concatenate(
        [jnp.full((offset,), -1, jnp.int32), segment_ids[0], jnp.full((half_span,), -1, jnp.int32)]
    )
    valid_pad = jnp.concatenate(
        [jnp.zeros((offset,), jnp.int32), valid_mask[0], jnp.zeros((half_span,), jnp.int32)]
    )
    query_pos = row_start - rim_rows + jnp.arange(tokens + rim_rows, dtype=jnp.int32)
    key_pos = window_start - half_span + jnp.arange(window + 2 * half_span, dtype=jnp.int32)
    query_seg = lax.dynamic_slice_in_dim(
        segment_pad, row_start - rim_rows + offset, tokens + rim_rows
    )
    key_seg = lax.dynamic_slice_in_dim(
        segment_pad, window_start - half_span + offset, window + 2 * half_span
    )
    query_live = lax.dynamic_slice_in_dim(
        valid_pad, row_start - rim_rows + offset, tokens + rim_rows
    )
    key_live = lax.dynamic_slice_in_dim(
        valid_pad, window_start - half_span + offset, window + 2 * half_span
    )
    mask_ext = (
        (query_seg[:, None] == key_seg[None, :])
        & (key_pos[None, :] <= query_pos[:, None])
        & (query_live[:, None] > 0)
        & (key_live[None, :] > 0)
    ).astype(jnp.float32)
    mask_own = mask_ext[rim_rows:, half_span : half_span + window]
    row_valid = query_live[rim_rows:].astype(jnp.float32)[:, None]
    full_input, full_output = (
        lax.all_gather(input_weight, "seq", axis=0, tiled=True),
        lax.all_gather(output_weight, "seq", axis=0, tiled=True),
    )
    first_scale = rms_scale(resid_in)
    normed_in = (resid_in * first_scale * first_gain).astype(jnp.bfloat16)
    projected = jnp.dot(normed_in, full_input, preferred_element_type=jnp.float32).astype(
        jnp.bfloat16
    )
    query = projected[:, :model_width]
    keys_values = projected[:, model_width:]
    query_rim = from_behind(query[tokens - rim_rows :], "seq", 1)
    query_ext = jnp.concatenate([query_rim, query], axis=0)
    pieces = [keys_values]
    for distance in range(1, REACH):
        pieces.append(from_behind(keys_values, "seq", distance))
    window_rows = jnp.concatenate(pieces[::-1], axis=0)
    key_ext = jnp.pad(window_rows[:, :model_width], ((half_span, half_span), (0, 0)))
    value_window = window_rows[:, model_width:]

    def split_heads(values):
        return values.reshape(values.shape[0], groups, 2, head_dim).transpose(1, 0, 2, 3)

    def merge_heads(values):
        return values.transpose(1, 0, 2, 3).reshape(values.shape[1], model_width)

    query_groups = split_heads(query_ext)
    key_groups = split_heads(key_ext)
    value_groups = split_heads(value_window)
    kernel_groups = conv_kernel.reshape(groups, 2, conv_kernel.shape[1], conv_kernel.shape[2])
    result_groups, lse_groups = lax.map(
        lambda operands: attend_group(operands, mask_ext, mask_own, row_valid, score_scale),
        (query_groups, key_groups, value_groups, kernel_groups, head_mix),
    )
    attended = merge_heads(result_groups)
    shaped = attended.reshape(tokens, head_count, head_dim)
    centred = shaped - jnp.mean(shaped, axis=-1, keepdims=True)
    inv_std = lax.rsqrt(jnp.mean(centred * centred, axis=-1, keepdims=True) + EPS)
    unit_heads = centred * inv_std
    unit = unit_heads.reshape(tokens, model_width)
    normed = (unit * group_gain).astype(jnp.bfloat16)
    branch = jnp.dot(normed, full_output, preferred_element_type=jnp.float32)
    resid = resid_in + row_valid * branch
    second_scale = rms_scale(resid)
    normed_mid = (resid * second_scale * second_gain).astype(jnp.bfloat16)
    dmlp = (row_valid * grad_out).astype(jnp.bfloat16)
    contract_rows = (((0,), (0,)), ((), ()))
    inputs_all = lax.all_gather(normed_mid, "seq", axis=0, tiled=True)
    gate = jnp.dot(inputs_all, gate_weight, preferred_element_type=jnp.float32)
    up_proj = jnp.dot(inputs_all, up_weight, preferred_element_type=jnp.float32)
    hidden = (jax.nn.silu(gate) * up_proj).astype(jnp.bfloat16)
    mlp = lax.psum_scatter(
        jnp.dot(hidden, down_weight, preferred_element_type=jnp.float32).astype(jnp.bfloat16),
        "seq",
        scatter_dimension=0,
        tiled=True,
    ).astype(jnp.float32)
    result = resid + row_valid * mlp
    dmlp_all = lax.all_gather(dmlp, "seq", axis=0, tiled=True)
    dhidden = jnp.dot(dmlp_all, down_weight.T, preferred_element_type=jnp.float32)
    sigmoid_gate = jax.nn.sigmoid(gate)
    gate_grad = (dhidden * up_proj * sigmoid_gate * (1.0 + gate * (1.0 - sigmoid_gate))).astype(
        jnp.bfloat16
    )
    up_grad = (dhidden * gate * sigmoid_gate).astype(jnp.bfloat16)
    grad_down = lax.dot_general(hidden, dmlp_all, contract_rows, preferred_element_type=jnp.float32)
    grad_gate = lax.dot_general(
        inputs_all, gate_grad, contract_rows, preferred_element_type=jnp.float32
    )
    grad_up = lax.dot_general(
        inputs_all, up_grad, contract_rows, preferred_element_type=jnp.float32
    )
    dmid = lax.psum_scatter(
        (
            jnp.dot(gate_grad, gate_weight.T, preferred_element_type=jnp.float32)
            + jnp.dot(up_grad, up_weight.T, preferred_element_type=jnp.float32)
        ).astype(jnp.bfloat16),
        "seq",
        scatter_dimension=0,
        tiled=True,
    ).astype(jnp.float32)
    second_part = jnp.sum(dmid * resid * second_scale, axis=0)
    dresid = grad_out + norm_back(dmid, resid, second_scale, second_gain)
    dbranch = (row_valid * dresid).astype(jnp.bfloat16)
    whole_output_grad = lax.dot_general(
        normed, dbranch, contract_rows, preferred_element_type=jnp.float32
    )
    dnormed = jnp.dot(dbranch, full_output.T, preferred_element_type=jnp.float32)
    group_part = jnp.sum(dnormed * unit, axis=0)
    dunit = (dnormed * group_gain).reshape(tokens, head_count, head_dim)
    dshaped = inv_std * (
        dunit
        - jnp.mean(dunit, axis=-1, keepdims=True)
        - unit_heads * jnp.mean(dunit * unit_heads, axis=-1, keepdims=True)
    )
    dattended = dshaped.reshape(tokens, model_width).astype(jnp.bfloat16)
    dquery_g, dkey_g, dvalue_g, dkernel_g, dmixing = lax.map(
        lambda operands: attend_group_back(operands, mask_ext, mask_own, score_scale),
        (
            query_groups,
            key_groups,
            value_groups,
            kernel_groups,
            head_mix,
            split_heads(dattended),
            lse_groups,
        ),
    )
    dquery_ext = merge_heads(dquery_g)
    dkey_window = merge_heads(dkey_g)[half_span : half_span + window]
    dvalue_window = merge_heads(dvalue_g)
    dpair_window = jnp.concatenate([dkey_window, dvalue_window], axis=1)
    dpair = dpair_window[(REACH - 1) * tokens :]
    for distance in range(1, REACH):
        block_first = (REACH - 1 - distance) * tokens
        dpair = dpair + from_behind(
            dpair_window[block_first : block_first + tokens].astype(jnp.bfloat16), "seq", -distance
        ).astype(jnp.float32)
    rim_grad = from_behind(dquery_ext[:rim_rows], "seq", -1)
    dquery_own = dquery_ext[rim_rows:]
    dquery_own = jnp.concatenate(
        [dquery_own[: tokens - rim_rows], dquery_own[tokens - rim_rows :] + rim_grad], axis=0
    )
    dprojected = jnp.concatenate([dquery_own, dpair], axis=1).astype(jnp.bfloat16)
    whole_input_grad = lax.dot_general(
        normed_in, dprojected, contract_rows, preferred_element_type=jnp.float32
    )
    dnormin = jnp.dot(dprojected, full_input.T, preferred_element_type=jnp.float32)
    first_part = jnp.sum(dnormin * resid_in * first_scale, axis=0)
    grad_in = dresid + norm_back(dnormin, resid_in, first_scale, first_gain)
    input_shard, output_shard = (
        lax.psum_scatter(
            whole_input_grad.astype(jnp.bfloat16), "seq", scatter_dimension=0, tiled=True
        ).astype(jnp.float32),
        lax.psum_scatter(
            whole_output_grad.astype(jnp.bfloat16), "seq", scatter_dimension=0, tiled=True
        ).astype(jnp.float32),
    )
    kernel_part = dkernel_g.reshape(head_count, conv_kernel.shape[1], conv_kernel.shape[2])
    grad_kernel, grad_mix, grad_first, grad_second, grad_group = lax.psum(
        (kernel_part, dmixing, first_part, second_part, group_part), ("rep", "seq")
    )
    grad_input_w, grad_output_w, grad_gate, grad_up, grad_down = (
        lax.psum(input_shard.astype(jnp.bfloat16), "rep").astype(jnp.float32),
        lax.psum(output_shard.astype(jnp.bfloat16), "rep").astype(jnp.float32),
        lax.psum(grad_gate.astype(jnp.bfloat16), "rep").astype(jnp.float32),
        lax.psum(grad_up.astype(jnp.bfloat16), "rep").astype(jnp.float32),
        lax.psum(grad_down.astype(jnp.bfloat16), "rep").astype(jnp.float32),
    )
    return (
        result.astype(jnp.bfloat16)[None],
        grad_in.astype(jnp.bfloat16)[None],
        grad_input_w,
        grad_output_w,
        grad_kernel,
        grad_mix,
        grad_first,
        grad_second,
        grad_group,
        grad_gate,
        grad_up,
        grad_down,
    )


def solution(mesh):
    in_specs = (
        P("rep", "seq", None),
        P("rep", None),
        P("rep", None),
        P("seq", None),
        P("seq", None),
        P(),
        P(),
        P(),
        P(),
        P(),
        P(None, "seq"),
        P(None, "seq"),
        P("seq", None),
        P("rep", "seq", None),
    )
    out_specs = (
        P("rep", "seq", None),
        P("rep", "seq", None),
        P("seq", None),
        P("seq", None),
        P(),
        P(),
        P(),
        P(),
        P(),
        P(None, "seq"),
        P(None, "seq"),
        P("seq", None),
    )
    return jax.shard_map(
        on_device, mesh=mesh, in_specs=in_specs, out_specs=out_specs, check_vma=False
    )
```

profile of v0, /device:TPU:0, one launch (start us, length us, event | category | flops | bytes accessed | tf_op | source)
XLA Modules:
  0.0 4016.5 jit_solution(8021908718773649853)
XLA Ops:
  9.3 132.8 %all-gather.5.cloned.1.call-done = bf16[1536,4608]{1,0:T(8,128)(2,1)} async-done(((bf16[192,4608]{1,0:T(8,128)(2,1)}), bf16[1536,4608]{1,0:T(8,128)(2,1)}) %all-gather.5.cloned.1.call-update) | async-done | bytes 14155792 | tf_op jit(solution)/shard_map/all_gather | solution.py:209
  178.6 39.8 collective-permute-done.1
  218.4 47.0 %collective-permute-done = bf16[256,3072]{1,0:T(8,128)(2,1)} collective-permute-done((bf16[256,3072]{1,0:T(8,128)(2,1)}, bf16[256,3072]{1,0:T(8,128)(2,1)}, u32[]{:S(2)}, u32[]{:S(2)}) %collective-permute-start) | collective-permute-done | bytes 1572896 | tf_op jit(solution)/shard_map/ppermute | solution.py:14
  286.9 341.3 %while.34 = (s32[]{:T(128)}, f32[8,256,2,96]{1,3,2,0:T(8,128)S(1)}, f32[8,2,256,1]{2,1,3,0:T(2,128)}, bf16[8,1024,2,96]{1,3,2,0:T(8,128)(2,1)}, f32[8,2,2]{2,1,0...) while((s32[]{:T(128)}, f32[8,256,2,96]{1,3,2,0:T(8,128)S(1)}, ...), condition=%wide.region_4.5_spmd.clone, body=%wide.region_1.4_spmd.clone.sunk | while | flops 281692032 | bytes 160720624 | solution.py:238
  652.1 102.0 %all-gather.9.cloned.1.call-done = bf16[2048,1536]{1,0:T(8,128)(2,1)} async-done(((bf16[256,1536]{1,0:T(8,128)(2,1)}), bf16[2048,1536]{1,0:T(8,128)(2,1)}) %all-gather.9.cloned.1.call-update) | async-done | bytes 6291472 | tf_op jit(solution)/shard_map/all_gather | solution.py:255
  767.9 51.8 %all-gather.11.cloned.1.call-done = bf16[2048,1536]{1,0:T(8,128)(2,1)} async-done(((bf16[256,1536]{1,0:T(8,128)(2,1)}), bf16[2048,1536]{1,0:T(8,128)(2,1)}) %all-gather.11.cloned.1.call-update) | async-done | bytes 6291472 | tf_op jit(solution)/shard_map/all_gather | solution.py:266
  848.9 61.1 %reduce-scatter.7.cloned.1.call-done = bf16[256,1536]{1,0:T(8,128)(2,1)} async-done(((bf16[2048,1536]{1,0:T(8,128)(2,1)}), bf16[256,1536]{1,0:T(8,128)(2,1)}) %reduce-scatter.7.cloned.1.call-update) | async-done | bytes 786448 | tf_op jit(solution)/shard_map/reduce_scatter | solution.py:280
  912.2 68.2 %reduce-scatter.5.cloned.1.call-done = bf16[256,1536]{1,0:T(8,128)(2,1)} async-done(((bf16[2048,1536]{1,0:T(8,128)(2,1)}), bf16[256,1536]{1,0:T(8,128)(2,1)}) %reduce-scatter.5.cloned.1.call-update) | async-done | bytes 786448 | tf_op jit(solution)/shard_map/reduce_scatter | solution.py:259
  1008.2 2550.7 %while.35 = (s32[]{:T(128)}, f32[8,261,2,96]{3,1,2,0:T(8,128)}, f32[8,1034,2,96]{1,3,2,0:T(8,128)}, f32[8,1024,2,96]{1,3,2,0:T(8,128)}, f32[8,2,6,11]{3,1,0,2:T(...) while((s32[]{:T(128)}, f32[8,261,2,96]{3,1,2,0:T(8,128)}, ...), condition=%wide.region_83.84_spmd.clone, body=%wide.region_13.83_spmd.clone.sunk | while | flops 1772737280 | bytes 370601792 | solution.py:304
  1041.3 36.7 multiply_reduce_fusion.77
  1163.3 124.6 %multiply_multiply_fusion.4 = f32[2,261,1034]{2,1,0:T(8,128)S(1)} fusion(f32[2,256,1024]{2,1,0:T(8,128)} %get-tuple-element.1464, f32[261,1034]{1,0:T(8,128)} %fusion.360, f32[2]{0:T(128)} %get-tuple-element.1396, f32[2]{0:T(128)} %get-tuple-element.1397, f32[2]{0:T(128)} %get-tuple-element.1398, f32[2]{0:T(128)} %get-tuple-element.1399, ...), kind=kLoop, calls=%fused_computation.436.clone.1 | loop fusion | flops 71786448 | bytes 5336168 | tf_op jit(solution)/shard_map/while/body/eval_jaxpr/mul | solution.py:121
  1478.6 124.6 %multiply_multiply_fusion.4 = f32[2,261,1034]{2,1,0:T(8,128)S(1)} fusion(f32[2,256,1024]{2,1,0:T(8,128)} %get-tuple-element.1464, f32[261,1034]{1,0:T(8,128)} %fusion.360, f32[2]{0:T(128)} %get-tuple-element.1396, f32[2]{0:T(128)} %get-tuple-element.1397, f32[2]{0:T(128)} %get-tuple-element.1398, f32[2]{0:T(128)} %get-tuple-element.1399, ...), kind=kLoop, calls=%fused_computation.436.clone.1 | loop fusion | flops 71786448 | bytes 5336168 | tf_op jit(solution)/shard_map/while/body/eval_jaxpr/mul | solution.py:121
  1671.8 36.7 multiply_reduce_fusion.77
  1793.8 124.6 %multiply_multiply_fusion.4 = f32[2,261,1034]{2,1,0:T(8,128)S(1)} fusion(f32[2,256,1024]{2,1,0:T(8,128)} %get-tuple-element.1464, f32[261,1034]{1,0:T(8,128)} %fusion.360, f32[2]{0:T(128)} %get-tuple-element.1396, f32[2]{0:T(128)} %get-tuple-element.1397, f32[2]{0:T(128)} %get-tuple-element.1398, f32[2]{0:T(128)} %get-tuple-element.1399, ...), kind=kLoop, calls=%fused_computation.436.clone.1 | loop fusion | flops 71786448 | bytes 5336168 | tf_op jit(solution)/shard_map/while/body/eval_jaxpr/mul | solution.py:121
  2109.1 124.6 %multiply_multiply_fusion.4 = f32[2,261,1034]{2,1,0:T(8,128)S(1)} fusion(f32[2,256,1024]{2,1,0:T(8,128)} %get-tuple-element.1464, f32[261,1034]{1,0:T(8,128)} %fusion.360, f32[2]{0:T(128)} %get-tuple-element.1396, f32[2]{0:T(128)} %get-tuple-element.1397, f32[2]{0:T(128)} %get-tuple-element.1398, f32[2]{0:T(128)} %get-tuple-element.1399, ...), kind=kLoop, calls=%fused_computation.436.clone.1 | loop fusion | flops 71786448 | bytes 5336168 | tf_op jit(solution)/shard_map/while/body/eval_jaxpr/mul | solution.py:121
  2424.4 124.6 %multiply_multiply_fusion.4 = f32[2,261,1034]{2,1,0:T(8,128)S(1)} fusion(f32[2,256,1024]{2,1,0:T(8,128)} %get-tuple-element.1464, f32[261,1034]{1,0:T(8,128)} %fusion.360, f32[2]{0:T(128)} %get-tuple-element.1396, f32[2]{0:T(128)} %get-tuple-element.1397, f32[2]{0:T(128)} %get-tuple-element.1398, f32[2]{0:T(128)} %get-tuple-element.1399, ...), kind=kLoop, calls=%fused_computation.436.clone.1 | loop fusion | flops 71786448 | bytes 5336168 | tf_op jit(solution)/shard_map/while/body/eval_jaxpr/mul | solution.py:121
  2617.6 36.7 multiply_reduce_fusion.77
  2739.6 124.6 %multiply_multiply_fusion.4 = f32[2,261,1034]{2,1,0:T(8,128)S(1)} fusion(f32[2,256,1024]{2,1,0:T(8,128)} %get-tuple-element.1464, f32[261,1034]{1,0:T(8,128)} %fusion.360, f32[2]{0:T(128)} %get-tuple-element.1396, f32[2]{0:T(128)} %get-tuple-element.1397, f32[2]{0:T(128)} %get-tuple-element.1398, f32[2]{0:T(128)} %get-tuple-element.1399, ...), kind=kLoop, calls=%fused_computation.436.clone.1 | loop fusion | flops 71786448 | bytes 5336168 | tf_op jit(solution)/shard_map/while/body/eval_jaxpr/mul | solution.py:121
  3054.9 124.6 %multiply_multiply_fusion.4 = f32[2,261,1034]{2,1,0:T(8,128)S(1)} fusion(f32[2,256,1024]{2,1,0:T(8,128)} %get-tuple-element.1464, f32[261,1034]{1,0:T(8,128)} %fusion.360, f32[2]{0:T(128)} %get-tuple-element.1396, f32[2]{0:T(128)} %get-tuple-element.1397, f32[2]{0:T(128)} %get-tuple-element.1398, f32[2]{0:T(128)} %get-tuple-element.1399, ...), kind=kLoop, calls=%fused_computation.436.clone.1 | loop fusion | flops 71786448 | bytes 5336168 | tf_op jit(solution)/shard_map/while/body/eval_jaxpr/mul | solution.py:121
  3370.2 124.6 %multiply_multiply_fusion.4 = f32[2,261,1034]{2,1,0:T(8,128)S(1)} fusion(f32[2,256,1024]{2,1,0:T(8,128)} %get-tuple-element.1464, f32[261,1034]{1,0:T(8,128)} %fusion.360, f32[2]{0:T(128)} %get-tuple-element.1396, f32[2]{0:T(128)} %get-tuple-element.1397, f32[2]{0:T(128)} %get-tuple-element.1398, f32[2]{0:T(128)} %get-tuple-element.1399, ...), kind=kLoop, calls=%fused_computation.436.clone.1 | loop fusion | flops 71786448 | bytes 5336168 | tf_op jit(solution)/shard_map/while/body/eval_jaxpr/mul | solution.py:121
  3620.5 38.8 collective-permute-done.6
  3693.2 147.7 %reduce-scatter.9.cloned.1.call-done = bf16[192,4608]{1,0:T(8,128)(2,1)} async-done(((bf16[1536,4608]{1,0:T(8,128)(2,1)}), bf16[192,4608]{1,0:T(8,128)(2,1)}) %reduce-scatter.9.cloned.1.call-update) | async-done | bytes 1769488 | tf_op jit(solution)/shard_map/reduce_scatter | solution.py:339
  3853.7 40.1 all-reduce.2
  3898.0 100.9 %all-reduce.6.cloned.1.call-done = (bf16[192,4608]{1,0:T(8,128)(2,1)}, bf16[192,1536]{1,0:T(8,128)(2,1)}, bf16[1536,512]{1,0:T(8,128)(2,1)}, bf16[1536,512]{1,0:T(8,128)(2,1)}, bf16[512,1536]{1,0:T(8,128)(2,1)}) async-done(((bf16[192,4608]{1,0:T(8,128)(2,1)}, bf16[192,1536]{1,0:T(8,128)(2,1)}, bf16[1536,512]{1,0:T(8,128)(2,1)}, bf16[1536,512]{1,0:T(8,128)(2,1)}, bf16[512,1536]{1,0:T(8,128)(2,1)}), ...) | async-done | bytes 7077904 | tf_op jit(solution)/shard_map/psum | solution.py:351
  (1999 shorter events, 2029.6 us)
Async XLA Ops:
  7.2 812.5 %copy-start = (bf16[512,1536]{1,0:T(8,128)(2,1)S(1)}, bf16[512,1536]{1,0:T(8,128)(2,1)}, u32[]{:S(2)}) copy-start(bf16[512,1536]{1,0:T(8,128)(2,1)} %param.30) | copy-start | bytes 4718596
  7.2 134.9 %copy-start.64 = (f32[1536]{0:T(1024)S(1)}, f32[1536]{0:T(1024)}, u32[]{:S(2)}) copy-start(f32[1536]{0:T(1024)} %param.25) | copy-start | bytes 18436
  7.2 134.8 %all-gather.5.cloned.1.call-start = ((), (), s32[]{:S(2)}) async-start(), calls=%async_computation.4 | async-start | bytes 15925248 | tf_op jit(solution)/shard_map/all_gather | solution.py:209
  8.0 634.8 %all-gather.7.cloned.1.call-start = ((), (), s32[]{:S(2)}) async-start(), calls=%async_computation.5 | async-start | bytes 5308416 | tf_op jit(solution)/shard_map/all_gather | solution.py:210
  9.3 142.0 %copy-start.72 = (f32[256]{0:T(256)}, f32[256]{0:T(256)S(1)}, u32[]{:S(2)}) copy-start(f32[256]{0:T(256)S(1)} %get-tuple-element.869) | copy-start | bytes 3076
  154.1 24.5 collective-permute-start.2
  157.4 61.1 %collective-permute-start.1 = (bf16[256,3072]{1,0:T(8,128)(2,1)}, bf16[256,3072]{1,0:T(8,128)(2,1)}, u32[]{:S(2)}, u32[]{:S(2)}) collective-permute-start(bf16[256,3072]{1,0:T(8,128)(2,1)} %slice.2477), channel_id=1, source_target_pairs={{0,2},{1,3},{2,4},{3,5},{4,6},{5,7},{8,10},{9,11},{10,12},{11,13},... | collective-permute-start | bytes 4718600 | tf_op jit(solution)/shard_map/ppermute | solution.py:14
  159.8 105.6 %collective-permute-start = (bf16[256,3072]{1,0:T(8,128)(2,1)}, bf16[256,3072]{1,0:T(8,128)(2,1)}, u32[]{:S(2)}, u32[]{:S(2)}) collective-permute-start(bf16[256,3072]{1,0:T(8,128)(2,1)} %slice.2477), channel_id=1, source_target_pairs={{0,3},{1,4},{2,5},{3,6},{4,7},{8,11},{9,12},{10,13},{11,14},{12,15... | collective-permute-start | bytes 4718600 | tf_op jit(solution)/shard_map/ppermute | solution.py:14
  162.3 591.8 %all-gather.9.cloned.1.call-start = ((), (), s32[]{:S(2)}) async-start(), calls=%async_computation.6 | async-start | bytes 7077888 | tf_op jit(solution)/shard_map/all_gather | solution.py:255
  165.4 3.6 collective-permute-start.3
  649.5 170.1 %all-gather.11.cloned.1.call-start = ((), (), s32[]{:S(2)}) async-start(), calls=%async_computation.8 | async-start | bytes 7077888 | tf_op jit(solution)/shard_map/all_gather | solution.py:266
  651.8 258.2 %reduce-scatter.7.cloned.1.call-start = ((), (), s32[]{:S(2)}) async-start(), calls=%async_computation.9 | async-start | bytes 7077888 | tf_op jit(solution)/shard_map/reduce_scatter | solution.py:280
  841.4 139.0 %reduce-scatter.5.cloned.1.call-start = ((), (), s32[]{:S(2)}) async-start(), calls=%async_computation.7 | async-start | bytes 7077888 | tf_op jit(solution)/shard_map/reduce_scatter | solution.py:259
  848.4 2844.7 %reduce-scatter.11.cloned.1.call-start = ((), (), s32[]{:S(2)}) async-start(), calls=%async_computation.11 | async-start | bytes 5308416 | tf_op jit(solution)/shard_map/reduce_scatter | solution.py:342
  1008.2 2832.7 %reduce-scatter.9.cloned.1.call-start = ((), (), s32[]{:S(2)}) async-start(), calls=%async_computation.10 | async-start | bytes 15925248 | tf_op jit(solution)/shard_map/reduce_scatter | solution.py:339
  3579.2 12.6 collective-permute-start.5
  3580.5 40.1 collective-permute-start.7
  3581.8 77.6 %collective-permute-start.6 = (bf16[256,3072]{0,1:T(8,128)(2,1)}, bf16[256,3072]{0,1:T(8,128)(2,1)}, u32[]{:S(2)}, u32[]{:S(2)}) collective-permute-start(bf16[256,3072]{0,1:T(8,128)(2,1)} %get-tuple-element.859), channel_id=1, source_target_pairs={{2,0},{3,1},{4,2},{5,3},{6,4},{7,5},{10,8},{11,9},{12,10},{13,11},... | collective-permute-start | bytes 4718600 | tf_op jit(solution)/shard_map/ppermute | solution.py:14
  3587.7 3.8 collective-permute-start.4
  3591.7 71.6 %copy-start.15 = (bf16[1,256,1536]{2,1,0:T(8,128)(2,1)S(1)}, bf16[1,256,1536]{2,1,0:T(8,128)(2,1)}, u32[]{:S(2)}) copy-start(bf16[1,256,1536]{2,1,0:T(8,128)(2,1)} %param.18) | copy-start | bytes 2359300
  3591.8 71.5 %copy-start.20 = (bf16[251,8,2,96]{0,3,2,1:T(8,128)(2,1)S(1)}, bf16[251,8,2,96]{0,3,2,1:T(8,128)(2,1)}, u32[]{:S(2)}) copy-start(bf16[251,8,2,96]{0,3,2,1:T(8,128)(2,1)} %slice.3701) | copy-start | bytes 2313220
  3591.8 71.5 %copy-start.65 = (f32[1536]{0:T(1024)S(1)}, f32[1536]{0:T(1024)}, u32[]{:S(2)}) copy-start(f32[1536]{0:T(1024)} %param.25) | copy-start | bytes 18436
  3591.8 71.5 %copy-start.73 = (f32[256]{0:T(256)S(1)}, f32[256]{0:T(256)}, u32[]{:S(2)}) copy-start(f32[256]{0:T(256)} %copy-done.72) | copy-start | bytes 3076
  3672.5 326.4 %all-reduce.6.cloned.1.call-start = ((), (), s32[]{:S(2)}) async-start(), calls=%async_computation.12 | async-start | bytes 14155776 | tf_op jit(solution)/shard_map/psum | solution.py:351
  (417 other events, 4098.7 us)
Sparse Core Ops, SparseCore 0:
  9.7 132.3 all-gather.4
  162.4 82.5 all-gather.6
  649.7 104.4 all-gather.8
  756.2 63.4 all-gather.10
  841.5 68.4 reduce-scatter.6
  912.1 68.1 reduce-scatter.4
  1008.3 53.3 reduce-scatter.10
  3672.7 168.1 reduce-scatter.8
  3846.3 152.5 all-reduce.5
where the time goes:
time: 4040 us; the launch traced here: 4020 us
  other arithmetic  2010 us (50%)
  local copies, waits for them, and re-layouts  853 us (21%)
  waiting for transfers between devices  821 us (20%)
  matrix products  225 us (6%)
    mul x8, other arithmetic, attend_group_back(): dlogits = convolve_back(dconv, kernel_g) * mask_ext * score_scale  997 us
    another operation x576, local copies, waits for them, and re-layouts, kernel_grads(): entries.append(jnp.stack(line_sums, axis=-1))  678 us
    reduce_sum x32, other arithmetic, kernel_grads(): line_sums.append(jnp.sum(grads * window_part, axis=(1, 2)))  334 us
    reduce_sum x8, other arithmetic, attend_group_back(): dconv = prob * (dprob - jnp.sum(prob * dprob, axis=-1, keepdims=True))  294 us
    reduce_max x8, other arithmetic, attend_group(): peak = jnp.max(jnp.where(allowed, conv, -1e+30), axis=-1, keepdims=True)  277 us
    ppermute x8, waiting for transfers between devices, from_behind(): return lax.ppermute(x, axis, pairs)  155 us
    reduce_scatter x1, waiting for transfers between devices, on_device(): lax.psum_scatter(whole_input_grad.astype(jnp.bfloat16), 'seq', scatter_di...  148 us
    all_gather x1, waiting for transfers between devices, on_device(): lax.all_gather(input_weight, 'seq', axis=0, tiled=True)  133 us
  transfers between devices with their start and end apart: 17, of which 12 were waited for; matrix products, arithmetic and copies ran while one was open for 74% of the time, Pallas kernels for 0%

commit v1 on v0

--- a/solution.py
+++ b/solution.py
@@ -348,7 +348,9 @@
         (kernel_part, dmixing, first_part, second_part, group_part), ("rep", "seq")
     )
     grad_input_w, grad_output_w, grad_gate, grad_up, grad_down = (
-        lax.psum(input_shard.astype(jnp.bfloat16), "rep").astype(jnp.float32),
+        jnp.sum(lax.all_gather(input_shard.astype(jnp.bfloat16), "rep"), axis=0).astype(
+            jnp.float32
+        ),
         lax.psum(output_shard.astype(jnp.bfloat16), "rep").astype(jnp.float32),
         lax.psum(grad_gate.astype(jnp.bfloat16), "rep").astype(jnp.float32),
         lax.psum(grad_up.astype(jnp.bfloat16), "rep").astype(jnp.float32),

time: 4040 us -> 3010 us (0.75)
  other arithmetic: 2010 us -> 1380 us
  local copies, waits for them, and re-layouts: 853 us -> 427 us
  waiting for transfers between devices: 821 us -> 862 us
    mul x8, other arithmetic: 997 us -> 367 us  [attend_group_back(): dlogits = convolve_back(dconv, kernel_g) * mask_ext * score_scale]
    another operation x576, local copies, waits for them, and re-layouts: 678 us -> 235 us  [kernel_grads(): entries.append(jnp.stack(line_sums, axis=-1))]
    all_gather x0 -> x1, waiting for transfers between devices: none -> 69.5 us  [on_device(): lax.all_gather(input_shard.astype(jnp.bfloat16), 'rep')]
  transfers between devices with their start and end apart: 17 -> 18, of which waited for: 12 -> 13; matrix products, arithmetic and copies ran while one was open for 74% -> 66% of each run, Pallas kernels for 0% -> 0%
where the time goes in v1:
time: 3010 us; the launch traced here: 3000 us
  other arithmetic  1380 us (46%)
  waiting for transfers between devices  862 us (29%)
  local copies, waits for them, and re-layouts  427 us (14%)
  matrix products  243 us (8%)
  blocking collectives  40.2 us (1%)
    mul x8, other arithmetic, attend_group_back(): dlogits = convolve_back(dconv, kernel_g) * mask_ext * score_scale  367 us
    reduce_sum x32, other arithmetic, kernel_grads(): line_sums.append(jnp.sum(grads * window_part, axis=(1, 2)))  335 us
    reduce_sum x8, other arithmetic, attend_group_back(): dconv = prob * (dprob - jnp.sum(prob * dprob, axis=-1, keepdims=True))  294 us
    reduce_max x8, other arithmetic, attend_group(): peak = jnp.max(jnp.where(allowed, conv, -1e+30), axis=-1, keepdims=True)  277 us
    another operation x576, local copies, waits for them, and re-layouts, kernel_grads(): entries.append(jnp.stack(line_sums, axis=-1))  235 us
    reduce_scatter x1, waiting for transfers between devices, on_device(): lax.psum_scatter(whole_input_grad.astype(jnp.bfloat16), 'seq', scatter_di...  156 us
    ppermute x8, waiting for transfers between devices, from_behind(): return lax.ppermute(x, axis, pairs)  147 us
    all_gather x1, waiting for transfers between devices, on_device(): lax.all_gather(input_weight, 'seq', axis=0, tiled=True)  133 us
  transfers between devices with their start and end apart: 18, of which 13 were waited for; matrix products, arithmetic and copies ran while one was open for 66% of the time, Pallas kernels for 0%

profile of v1, /device:TPU:0, one launch (start us, length us, event | category | flops | bytes accessed | tf_op | source)
XLA Modules:
  0.0 2997.7 jit_solution(7229267215168401925)
XLA Ops:
  9.3 132.8 %all-gather.7.cloned.1.call-done = bf16[1536,4608]{1,0:T(8,128)(2,1)} async-done(((bf16[192,4608]{1,0:T(8,128)(2,1)}), bf16[1536,4608]{1,0:T(8,128)(2,1)}) %all-gather.7.cloned.1.call-update) | async-done | bytes 14155792 | tf_op jit(solution)/shard_map/all_gather | solution.py:209
  209.0 52.4 %collective-permute-done.1 = bf16[256,3072]{1,0:T(8,128)(2,1)} collective-permute-done((bf16[256,3072]{1,0:T(8,128)(2,1)}, bf16[256,3072]{1,0:T(8,128)(2,1)}, u32[]{:S(2)}, u32[]{:S(2)}) %collective-permute-start.1) | collective-permute-done | bytes 1572896 | tf_op jit(solution)/shard_map/ppermute | solution.py:14
  282.9 336.9 %while.34 = (s32[]{:T(128)}, f32[8,256,2,96]{1,3,2,0:T(8,128)}, f32[8,2,256,1]{2,1,3,0:T(2,128)}, bf16[8,1024,2,96]{1,3,2,0:T(8,128)(2,1)}, f32[8,2,2]{2,1,0:T(2...) while((s32[]{:T(128)}, f32[8,256,2,96]{1,3,2,0:T(8,128)}, ...), condition=%wide.region_4.5_spmd.clone, body=%wide.region_1.4_spmd.clone.sunk | while | flops 281692032 | bytes 160720112 | solution.py:238
  647.1 103.4 %all-gather.11.cloned.1.call-done = bf16[2048,1536]{1,0:T(8,128)(2,1)} async-done(((bf16[256,1536]{1,0:T(8,128)(2,1)}), bf16[2048,1536]{1,0:T(8,128)(2,1)}) %all-gather.11.cloned.1.call-update) | async-done | bytes 6291472 | tf_op jit(solution)/shard_map/all_gather | solution.py:255
  764.2 51.8 %all-gather.13.cloned.1.call-done = bf16[2048,1536]{1,0:T(8,128)(2,1)} async-done(((bf16[256,1536]{1,0:T(8,128)(2,1)}), bf16[2048,1536]{1,0:T(8,128)(2,1)}) %all-gather.13.cloned.1.call-update) | async-done | bytes 6291472 | tf_op jit(solution)/shard_map/all_gather | solution.py:266
  844.9 61.5 %reduce-scatter.7.cloned.1.call-done = bf16[256,1536]{1,0:T(8,128)(2,1)} async-done(((bf16[2048,1536]{1,0:T(8,128)(2,1)}), bf16[256,1536]{1,0:T(8,128)(2,1)}) %reduce-scatter.7.cloned.1.call-update) | async-done | bytes 786448 | tf_op jit(solution)/shard_map/reduce_scatter | solution.py:280
  908.6 68.2 %reduce-scatter.5.cloned.1.call-done = bf16[256,1536]{1,0:T(8,128)(2,1)} async-done(((bf16[2048,1536]{1,0:T(8,128)(2,1)}), bf16[256,1536]{1,0:T(8,128)(2,1)}) %reduce-scatter.5.cloned.1.call-update) | async-done | bytes 786448 | tf_op jit(solution)/shard_map/reduce_scatter | solution.py:259
  1006.8 1488.4 %while.35 = (s32[]{:T(128)}, f32[8,261,2,96]{3,1,2,0:T(8,128)}, f32[8,1034,2,96]{1,3,2,0:T(8,128)}, f32[8,1024,2,96]{1,3,2,0:T(8,128)}, f32[8,2,6,11]{3,1,0,2:T(...) while((s32[]{:T(128)}, f32[8,261,2,96]{3,1,2,0:T(8,128)}, ...), condition=%wide.region_83.84_spmd.clone, body=%wide.region_13.83_spmd.clone.sunk | while | flops 1772737280 | bytes 383704672 | solution.py:304
  1018.0 36.8 %multiply_reduce_fusion.77 = (f32[2,256]{1,0:T(2,128)S(1)}, f32[2,256,1024]{2,1,0:T(8,128)S(1)}) fusion(f32[256,1024]{1,0:T(8,128)} %get-tuple-element.1391, f32[2]{0:T(128)} %get-tuple-element.1392, f32[256,1024]{1,0:T(8,128)S(1)} %get-tuple-element.1393, f32[2]{0:T(128)} %get-tuple-element.1394, f32[2,256]{1,0:T(2,128)S(1)} %fusion.359, ...), kind=kLoop, calls=%fused_computation.507.clone.1 | loop fusion | flops 72351232 | bytes 142873120 | tf_op jit(solution)/shard_map/while/body/eval_jaxpr/reduce_sum | solution.py:119
  1138.9 45.9 %multiply_multiply_fusion.4 = f32[2,261,1034]{2,1,0:T(8,128)} fusion(f32[2,256,1024]{2,1,0:T(8,128)S(1)} %copy-done.2, f32[261,1034]{1,0:T(8,128)S(1)} %fusion.360, f32[2]{0:T(128)S(1)} %get-tuple-element.1395, f32[2]{0:T(128)S(1)} %get-tuple-element.1396, f32[2]{0:T(128)S(1)} %get-tuple-element.1397, f32[2]{0:T(128)S(1)} %get-tuple-element.1398, ...), kind=kLoop, calls=%fused_computation.436.clone.1 | loop fusion | flops 71786448 | bytes 5336168 | tf_op jit(solution)/shard_map/while/body/eval_jaxpr/mul | solution.py:121
  1203.0 36.8 %multiply_reduce_fusion.77 = (f32[2,256]{1,0:T(2,128)S(1)}, f32[2,256,1024]{2,1,0:T(8,128)S(1)}) fusion(f32[256,1024]{1,0:T(8,128)} %get-tuple-element.1391, f32[2]{0:T(128)} %get-tuple-element.1392, f32[256,1024]{1,0:T(8,128)S(1)} %get-tuple-element.1393, f32[2]{0:T(128)} %get-tuple-element.1394, f32[2,256]{1,0:T(2,128)S(1)} %fusion.359, ...), kind=kLoop, calls=%fused_computation.507.clone.1 | loop fusion | flops 72351232 | bytes 142873120 | tf_op jit(solution)/shard_map/while/body/eval_jaxpr/reduce_sum | solution.py:119
  1323.9 45.9 %multiply_multiply_fusion.4 = f32[2,261,1034]{2,1,0:T(8,128)} fusion(f32[2,256,1024]{2,1,0:T(8,128)S(1)} %copy-done.2, f32[261,1034]{1,0:T(8,128)S(1)} %fusion.360, f32[2]{0:T(128)S(1)} %get-tuple-element.1395, f32[2]{0:T(128)S(1)} %get-tuple-element.1396, f32[2]{0:T(128)S(1)} %get-tuple-element.1397, f32[2]{0:T(128)S(1)} %get-tuple-element.1398, ...), kind=kLoop, calls=%fused_computation.436.clone.1 | loop fusion | flops 71786448 | bytes 5336168 | tf_op jit(solution)/shard_map/while/body/eval_jaxpr/mul | solution.py:121
  1508.9 45.9 %multiply_multiply_fusion.4 = f32[2,261,1034]{2,1,0:T(8,128)} fusion(f32[2,256,1024]{2,1,0:T(8,128)S(1)} %copy-done.2, f32[261,1034]{1,0:T(8,128)S(1)} %fusion.360, f32[2]{0:T(128)S(1)} %get-tuple-element.1395, f32[2]{0:T(128)S(1)} %get-tuple-element.1396, f32[2]{0:T(128)S(1)} %get-tuple-element.1397, f32[2]{0:T(128)S(1)} %get-tuple-element.1398, ...), kind=kLoop, calls=%fused_computation.436.clone.1 | loop fusion | flops 71786448 | bytes 5336168 | tf_op jit(solution)/shard_map/while/body/eval_jaxpr/mul | solution.py:121
  1573.0 36.8 %multiply_reduce_fusion.77 = (f32[2,256]{1,0:T(2,128)S(1)}, f32[2,256,1024]{2,1,0:T(8,128)S(1)}) fusion(f32[256,1024]{1,0:T(8,128)} %get-tuple-element.1391, f32[2]{0:T(128)} %get-tuple-element.1392, f32[256,1024]{1,0:T(8,128)S(1)} %get-tuple-element.1393, f32[2]{0:T(128)} %get-tuple-element.1394, f32[2,256]{1,0:T(2,128)S(1)} %fusion.359, ...), kind=kLoop, calls=%fused_computation.507.clone.1 | loop fusion | flops 72351232 | bytes 142873120 | tf_op jit(solution)/shard_map/while/body/eval_jaxpr/reduce_sum | solution.py:119
  1694.0 45.9 %multiply_multiply_fusion.4 = f32[2,261,1034]{2,1,0:T(8,128)} fusion(f32[2,256,1024]{2,1,0:T(8,128)S(1)} %copy-done.2, f32[261,1034]{1,0:T(8,128)S(1)} %fusion.360, f32[2]{0:T(128)S(1)} %get-tuple-element.1395, f32[2]{0:T(128)S(1)} %get-tuple-element.1396, f32[2]{0:T(128)S(1)} %get-tuple-element.1397, f32[2]{0:T(128)S(1)} %get-tuple-element.1398, ...), kind=kLoop, calls=%fused_computation.436.clone.1 | loop fusion | flops 71786448 | bytes 5336168 | tf_op jit(solution)/shard_map/while/body/eval_jaxpr/mul | solution.py:121
  1879.0 45.9 %multiply_multiply_fusion.4 = f32[2,261,1034]{2,1,0:T(8,128)} fusion(f32[2,256,1024]{2,1,0:T(8,128)S(1)} %copy-done.2, f32[261,1034]{1,0:T(8,128)S(1)} %fusion.360, f32[2]{0:T(128)S(1)} %get-tuple-element.1395, f32[2]{0:T(128)S(1)} %get-tuple-element.1396, f32[2]{0:T(128)S(1)} %get-tuple-element.1397, f32[2]{0:T(128)S(1)} %get-tuple-element.1398, ...), kind=kLoop, calls=%fused_computation.436.clone.1 | loop fusion | flops 71786448 | bytes 5336168 | tf_op jit(solution)/shard_map/while/body/eval_jaxpr/mul | solution.py:121
  2064.0 45.9 %multiply_multiply_fusion.4 = f32[2,261,1034]{2,1,0:T(8,128)} fusion(f32[2,256,1024]{2,1,0:T(8,128)S(1)} %copy-done.2, f32[261,1034]{1,0:T(8,128)S(1)} %fusion.360, f32[2]{0:T(128)S(1)} %get-tuple-element.1395, f32[2]{0:T(128)S(1)} %get-tuple-element.1396, f32[2]{0:T(128)S(1)} %get-tuple-element.1397, f32[2]{0:T(128)S(1)} %get-tuple-element.1398, ...), kind=kLoop, calls=%fused_computation.436.clone.1 | loop fusion | flops 71786448 | bytes 5336168 | tf_op jit(solution)/shard_map/while/body/eval_jaxpr/mul | solution.py:121
  2249.0 45.9 %multiply_multiply_fusion.4 = f32[2,261,1034]{2,1,0:T(8,128)} fusion(f32[2,256,1024]{2,1,0:T(8,128)S(1)} %copy-done.2, f32[261,1034]{1,0:T(8,128)S(1)} %fusion.360, f32[2]{0:T(128)S(1)} %get-tuple-element.1395, f32[2]{0:T(128)S(1)} %get-tuple-element.1396, f32[2]{0:T(128)S(1)} %get-tuple-element.1397, f32[2]{0:T(128)S(1)} %get-tuple-element.1398, ...), kind=kLoop, calls=%fused_computation.436.clone.1 | loop fusion | flops 71786448 | bytes 5336168 | tf_op jit(solution)/shard_map/while/body/eval_jaxpr/mul | solution.py:121
  2434.0 45.9 %multiply_multiply_fusion.4 = f32[2,261,1034]{2,1,0:T(8,128)} fusion(f32[2,256,1024]{2,1,0:T(8,128)S(1)} %copy-done.2, f32[261,1034]{1,0:T(8,128)S(1)} %fusion.360, f32[2]{0:T(128)S(1)} %get-tuple-element.1395, f32[2]{0:T(128)S(1)} %get-tuple-element.1396, f32[2]{0:T(128)S(1)} %get-tuple-element.1397, f32[2]{0:T(128)S(1)} %get-tuple-element.1398, ...), kind=kLoop, calls=%fused_computation.436.clone.1 | loop fusion | flops 71786448 | bytes 5336168 | tf_op jit(solution)/shard_map/while/body/eval_jaxpr/mul | solution.py:121
  2528.1 54.1 %collective-permute-done.6 = bf16[256,3072]{0,1:T(8,128)(2,1)} collective-permute-done((bf16[256,3072]{0,1:T(8,128)(2,1)}, bf16[256,3072]{0,1:T(8,128)(2,1)}, u32[]{:S(2)}, u32[]{:S(2)}) %collective-permute-start.6) | collective-permute-done | bytes 1572896 | tf_op jit(solution)/shard_map/ppermute | solution.py:14
  2621.2 156.1 %reduce-scatter.9.cloned.1.call-done = bf16[192,4608]{1,0:T(8,128)(2,1)} async-done(((bf16[1536,4608]{1,0:T(8,128)(2,1)}), bf16[192,4608]{1,0:T(8,128)(2,1)}) %reduce-scatter.9.cloned.1.call-update) | async-done | bytes 1769488 | tf_op jit(solution)/shard_map/reduce_scatter | solution.py:339
  2789.5 40.2 %all-reduce.2 = (f32[16,6,11]{2,0,1:T(8,128)S(1)}, f32[8,2,2]{0,2,1:T(2,128)}, f32[1536]{0:T(1024)}, f32[1536]{0:T(1024)}, f32[1536]{0:T(1024)}) all-reduce(f32[16,6,11]{2,0,1:T(8,128)} %bitcast.784, f32[8,2,2]{0,2,1:T(2,128)} %copy.255, f32[1536]{0:T(1024)} %get-tuple-element.619, ...), channel_id=1, replica_groups=mesh['rep'=4,'seq'=8] {'rep','seq'}, use_global_device_ids=true, to_apply=%region_89.90 | all-reduce | flops 5696 | bytes 45568 | tf_op jit(solution)/shard_map/psum | solution.py:347
  2833.9 70.9 %all-reduce.6.cloned.1.call-done = (bf16[192,1536]{1,0:T(8,128)(2,1)}, bf16[1536,512]{1,0:T(8,128)(2,1)}, bf16[1536,512]{1,0:T(8,128)(2,1)}, bf16[512,1536]{1,0:T(8,128)(2,1)}) async-done(((bf16[192,1536]{1,0:T(8,128)(2,1)}, bf16[1536,512]{1,0:T(8,128)(2,1)}, bf16[1536,512]{1,0:T(8,128)(2,1)}, bf16[512,1536]{1,0:T(8,128)(2,1)}), (bf16[192,1536]{1,0:T(8,128)(2,1)}, bf16[1536,512]{1,0:T(8,128)(2,1)}, ...) | async-done | bytes 5308432 | tf_op jit(solution)/shard_map/psum | solution.py:354
  2913.8 69.5 %all-gather.15.cloned.1.call-done = bf16[768,4608]{1,0:T(8,128)(2,1)} async-done(((bf16[192,4608]{1,0:T(8,128)(2,1)}), bf16[768,4608]{1,0:T(8,128)(2,1)}) %all-gather.15.cloned.1.call-update) | async-done | bytes 7077904 | tf_op jit(solution)/shard_map/all_gather | solution.py:351
  (2133 shorter events, 1628.3 us)
Async XLA Ops:
  7.2 808.9 %copy-start = (bf16[512,1536]{1,0:T(8,128)(2,1)S(1)}, bf16[512,1536]{1,0:T(8,128)(2,1)}, u32[]{:S(2)}) copy-start(bf16[512,1536]{1,0:T(8,128)(2,1)} %param.30) | copy-start | bytes 4718596
  7.2 134.9 %copy-start.69 = (f32[1536]{0:T(1024)S(1)}, f32[1536]{0:T(1024)}, u32[]{:S(2)}) copy-start(f32[1536]{0:T(1024)} %param.25) | copy-start | bytes 18436
  7.2 134.8 %all-gather.7.cloned.1.call-start = ((), (), s32[]{:S(2)}) async-start(), calls=%async_computation.4 | async-start | bytes 15925248 | tf_op jit(solution)/shard_map/all_gather | solution.py:209
  8.0 631.3 %all-gather.9.cloned.1.call-start = ((), (), s32[]{:S(2)}) async-start(), calls=%async_computation.5 | async-start | bytes 5308416 | tf_op jit(solution)/shard_map/all_gather | solution.py:210
  9.3 142.0 %copy-start.74 = (f32[256]{0:T(256)}, f32[256]{0:T(256)S(1)}, u32[]{:S(2)}) copy-start(f32[256]{0:T(256)S(1)} %get-tuple-element.868) | copy-start | bytes 3076
  154.1 55.0 %collective-permute-start = (bf16[256,3072]{1,0:T(8,128)(2,1)}, bf16[256,3072]{1,0:T(8,128)(2,1)}, u32[]{:S(2)}, u32[]{:S(2)}) collective-permute-start(bf16[256,3072]{1,0:T(8,128)(2,1)} %slice.2477), channel_id=1, source_target_pairs={{0,3},{1,4},{2,5},{3,6},{4,7},{8,11},{9,12},{10,13},{11,14},{12,15... | collective-permute-start | bytes 4718600 | tf_op jit(solution)/shard_map/ppermute | solution.py:14
  156.5 104.9 %collective-permute-start.1 = (bf16[256,3072]{1,0:T(8,128)(2,1)}, bf16[256,3072]{1,0:T(8,128)(2,1)}, u32[]{:S(2)}, u32[]{:S(2)}) collective-permute-start(bf16[256,3072]{1,0:T(8,128)(2,1)} %slice.2477), channel_id=1, source_target_pairs={{0,2},{1,3},{2,4},{3,5},{4,6},{5,7},{8,10},{9,11},{10,12},{11,13},... | collective-permute-start | bytes 4718600 | tf_op jit(solution)/shard_map/ppermute | solution.py:14
  161.3 100.1 %collective-permute-start.2 = (bf16[256,3072]{1,0:T(8,128)(2,1)}, bf16[256,3072]{1,0:T(8,128)(2,1)}, u32[]{:S(2)}, u32[]{:S(2)}) collective-permute-start(bf16[256,3072]{1,0:T(8,128)(2,1)} %slice.2477), channel_id=1, source_target_pairs={{0,1},{1,2},{2,3},{3,4},{4,5},{5,6},{6,7},{8,9},{9,10},{10,11},{11... | collective-permute-start | bytes 4718600 | tf_op jit(solution)/shard_map/ppermute | solution.py:14
  163.7 586.8 %all-gather.11.cloned.1.call-start = ((), (), s32[]{:S(2)}) async-start(), calls=%async_computation.6 | async-start | bytes 7077888 | tf_op jit(solution)/shard_map/all_gather | solution.py:255
  165.8 2.9 collective-permute-start.3
  645.9 170.1 %all-gather.13.cloned.1.call-start = ((), (), s32[]{:S(2)}) async-start(), calls=%async_computation.8 | async-start | bytes 7077888 | tf_op jit(solution)/shard_map/all_gather | solution.py:266
  647.0 259.3 %reduce-scatter.7.cloned.1.call-start = ((), (), s32[]{:S(2)}) async-start(), calls=%async_computation.9 | async-start | bytes 7077888 | tf_op jit(solution)/shard_map/reduce_scatter | solution.py:280
  837.8 139.0 %reduce-scatter.5.cloned.1.call-start = ((), (), s32[]{:S(2)}) async-start(), calls=%async_computation.7 | async-start | bytes 7077888 | tf_op jit(solution)/shard_map/reduce_scatter | solution.py:259
  844.8 1776.3 %reduce-scatter.11.cloned.1.call-start = ((), (), s32[]{:S(2)}) async-start(), calls=%async_computation.11 | async-start | bytes 5308416 | tf_op jit(solution)/shard_map/reduce_scatter | solution.py:342
  983.8 1793.5 %reduce-scatter.9.cloned.1.call-start = ((), (), s32[]{:S(2)}) async-start(), calls=%async_computation.10 | async-start | bytes 15925248 | tf_op jit(solution)/shard_map/reduce_scatter | solution.py:339
  2515.4 12.6 collective-permute-start.5
  2516.7 65.5 %collective-permute-start.6 = (bf16[256,3072]{0,1:T(8,128)(2,1)}, bf16[256,3072]{0,1:T(8,128)(2,1)}, u32[]{:S(2)}, u32[]{:S(2)}) collective-permute-start(bf16[256,3072]{0,1:T(8,128)(2,1)} %get-tuple-element.858), channel_id=1, source_target_pairs={{2,0},{3,1},{4,2},{5,3},{6,4},{7,5},{10,8},{11,9},{12,10},{13,11},... | collective-permute-start | bytes 4718600 | tf_op jit(solution)/shard_map/ppermute | solution.py:14
  2518.0 69.1 %collective-permute-start.7 = (bf16[256,3072]{0,1:T(8,128)(2,1)}, bf16[256,3072]{0,1:T(8,128)(2,1)}, u32[]{:S(2)}, u32[]{:S(2)}) collective-permute-start(bf16[256,3072]{0,1:T(8,128)(2,1)} %get-tuple-element.857), channel_id=1, source_target_pairs={{3,0},{4,1},{5,2},{6,3},{7,4},{11,8},{12,9},{13,10},{14,11},{15,12... | collective-permute-start | bytes 4718600 | tf_op jit(solution)/shard_map/ppermute | solution.py:14
  2524.0 3.8 collective-permute-start.4
  2528.0 63.1 %copy-start.18 = (bf16[1,256,1536]{2,1,0:T(8,128)(2,1)S(1)}, bf16[1,256,1536]{2,1,0:T(8,128)(2,1)}, u32[]{:S(2)}) copy-start(bf16[1,256,1536]{2,1,0:T(8,128)(2,1)} %param.18) | copy-start | bytes 2359300
  2528.0 63.1 %copy-start.24 = (bf16[251,8,2,96]{0,3,2,1:T(8,128)(2,1)S(1)}, bf16[251,8,2,96]{0,3,2,1:T(8,128)(2,1)}, u32[]{:S(2)}) copy-start(bf16[251,8,2,96]{0,3,2,1:T(8,128)(2,1)} %slice.3701) | copy-start | bytes 2313220
  2600.4 304.4 %all-reduce.6.cloned.1.call-start = ((), (), s32[]{:S(2)}) async-start(), calls=%async_computation.13 | async-start | bytes 10616832 | tf_op jit(solution)/shard_map/psum | solution.py:354
  2621.1 156.2 %copy-start.83 = (f32[8,2,2]{2,1,0:T(2,128)S(1)}, f32[8,2,2]{2,1,0:T(2,128)}, u32[]{:S(2)}) copy-start(f32[8,2,2]{2,1,0:T(2,128)} %get-tuple-element.270) | copy-start | bytes 388
  2621.1 362.1 %all-gather.15.cloned.1.call-start = ((), (), s32[]{:S(2)}) async-start(), calls=%async_computation.12 | async-start | bytes 8847360 | tf_op jit(solution)/shard_map/all_gather | solution.py:351
  (483 other events, 4302.4 us)
Sparse Core Ops, SparseCore 0:
  9.7 132.3 all-gather.6
  163.9 82.5 all-gather.8
  646.0 104.4 all-gather.10
  752.6 63.3 all-gather.12
  837.9 68.4 reduce-scatter.6
  908.5 68.1 reduce-scatter.4
  984.0 53.3 reduce-scatter.10
  2600.5 176.7 reduce-scatter.8
  2782.2 122.5 all-reduce.5
  2906.5 76.6 all-gather.14
